TPU v7x, 512 devices: a whole 4x8x8 slice. The times are simulated.
512 devices in a mesh: seq: 64 (over z, x, y_hi), dp: 8 (over y_lo, core).
Axes of the slice: x: 4, y: 8 (y_hi: 2, y_lo: 4; y = y_hi * 4 + y_lo), z: 8, core: 2. Of those that a mesh axis runs over, the one named last changes fastest.
Arguments:
- query_in: bfloat16 [16384, 2048], P('seq', 'dp'), may hold values from -6 to 6
- key_in: bfloat16 [16384, 2048], P('seq', 'dp'), may hold values from -6 to 6
- value_in: bfloat16 [16384, 2048], P('seq', 'dp'), may hold values from -6 to 6
- filters: bfloat16 [16, 2048], P(None, 'dp'), may hold values from -0.125 to 0.125
- out_weight: bfloat16 [2048, 2048], P('dp'), may hold values from -0.125 to 0.125
- grad_mixed: bfloat16 [16384, 2048], P('seq', 'dp'), may hold values from -16 to 16
Outputs:
- grad_query: bfloat16 [16384, 2048], P('seq', 'dp')
- grad_key: bfloat16 [16384, 2048], P('seq', 'dp')
- grad_value: bfloat16 [16384, 2048], P('seq', 'dp')
- grad_weight: float32 [2048, 2048], P('dp', 'seq')
- grad_filters: float32 [16, 2048], P('dp', 'seq')
All inputs are finite; a program needn't handle non-finite values.
Results may differ from a plain program's by a relative error of at most 0.0049.
Values may be sent and summed in bfloat16 or wider, within the bound.
No kernel may reach another device: no remote copies, remote signals or barrier semaphores. Data moves between devices by JAX's collectives and lax.ppermute only.
A program may use at most 64 MiB of HBM per device.

v0:
```python
import jax
import jax.numpy as jnp
from jax import lax
from jax.sharding import PartitionSpec as P

NUM_FILTERS = 16


def from_behind(block, axis, distance):
    devices = range(lax.axis_size(axis))
    route = [(i - distance, i) for i in devices if i - distance in devices]
    return lax.ppermute(block, axis, route)


def band_matrix(vector, row_count, col_count):
    period = vector.shape[0]
    tiled = jnp.tile(vector, (row_count,))[: row_count * (period - 1)]
    return tiled.reshape(row_count, period - 1)[:, :col_count]


def input_chain(own_shard, reach_count, hop_count):
    tok_rows, col_width = own_shard.shape
    stored = jnp.zeros((reach_count, tok_rows, col_width), own_shard.dtype)

    def input_advance(step_index, carried):
        moving, stored = carried
        moving = from_behind(moving, "seq", 1)
        stored = lax.dynamic_update_index_in_dim(stored, moving, reach_count - 1 - step_index, 0)
        return (moving, stored)

    moving, stored = lax.fori_loop(0, hop_count, input_advance, (own_shard, stored))
    return jnp.concatenate([stored.reshape(reach_count * tok_rows, col_width), own_shard], 0)


def grad_chain(own_shard, reach_count, hop_count):
    tok_rows, col_width = own_shard.shape
    stored = jnp.zeros((reach_count, tok_rows, col_width), own_shard.dtype)

    def grad_advance(step_index, carried):
        moving, stored = carried
        moving = from_behind(moving, "seq", -1)
        stored = lax.dynamic_update_index_in_dim(stored, moving, step_index, 0)
        return (moving, stored)

    moving, stored = lax.fori_loop(0, hop_count, grad_advance, (own_shard, stored))
    return jnp.concatenate([own_shard, stored.reshape(reach_count * tok_rows, col_width)], 0)


def per_device(query_in, key_in, value_in, filters, out_weight, grad_mixed):
    tok_rows, local_width = query_in.shape
    dp_count = lax.axis_size("dp")
    seq_count = lax.axis_size("seq")
    filter_len = filters.shape[1] * dp_count
    local_filters = NUM_FILTERS // dp_count
    group_width = local_width // local_filters
    reach_count = filter_len // tok_rows
    hop_count = min(reach_count, seq_count - 1)
    span_rows = filter_len + tok_rows
    period = span_rows + tok_rows
    all_taps = lax.all_gather(filters, "dp", axis=1, tiled=True)
    owned_taps = lax.dynamic_slice_in_dim(
        all_taps, lax.axis_index("dp") * local_filters, local_filters, 0
    )
    products = (key_in.astype(jnp.float32) * value_in.astype(jnp.float32)).astype(jnp.bfloat16)
    window_in = input_chain(products, reach_count, hop_count)
    head_zeros = jnp.zeros((local_filters, 1), jnp.bfloat16)
    tail_zeros = jnp.zeros((local_filters, period - 1 - filter_len), jnp.bfloat16)
    forward_vectors = jnp.concatenate([head_zeros, owned_taps[:, ::-1], tail_zeros], 1)
    after_zeros = jnp.zeros((local_filters, period - filter_len), jnp.bfloat16)
    backward_vectors = jnp.concatenate([owned_taps, after_zeros], 1)
    conv_parts = []
    for group_index in range(local_filters):
        forward_band = band_matrix(forward_vectors[group_index], tok_rows, span_rows)
        window_part = window_in[:, group_index * group_width : (group_index + 1) * group_width]
        conv_parts.append(jnp.dot(forward_band, window_part, preferred_element_type=jnp.float32))
    conv_out = jnp.concatenate(conv_parts, 1)
    gated = (query_in.astype(jnp.float32) * conv_out).astype(jnp.bfloat16)
    block_in = lax.all_gather(grad_mixed, "dp", axis=1, tiled=True)
    grad_part = lax.dot_general(
        block_in, out_weight, (((1,), (1,)), ((), ())), preferred_element_type=jnp.float32
    )
    block_grad = lax.dot_general(
        gated, block_in, (((0,), (0,)), ((), ())), preferred_element_type=jnp.float32
    )
    grad_query = (grad_part * conv_out).astype(jnp.bfloat16)
    grad_conv = (grad_part * query_in.astype(jnp.float32)).astype(jnp.bfloat16)
    window_grad = grad_chain(grad_conv, reach_count, hop_count)
    grad_parts = []
    filter_rows = []
    for group_index in range(local_filters):
        low_col = group_index * group_width
        backward_band = band_matrix(backward_vectors[group_index], tok_rows, span_rows)
        grad_window = window_grad[:, low_col : low_col + group_width]
        grad_parts.append(jnp.dot(backward_band, grad_window, preferred_element_type=jnp.float32))
        own_grads = grad_conv[:, low_col : low_col + group_width]
        window_part = window_in[:, low_col : low_col + group_width]
        lagged = lax.dot_general(
            own_grads, window_part, (((1,), (1,)), ((), ())), preferred_element_type=jnp.float32
        )
        flattened = jnp.pad(lagged.reshape(tok_rows * span_rows), (0, tok_rows))
        skewed = flattened.reshape(tok_rows, span_rows + 1)
        diagonal_sums = jnp.sum(skewed, axis=0)
        filter_rows.append(diagonal_sums[1 : filter_len + 1][::-1])
    grad_products = jnp.concatenate(grad_parts, 1)
    grad_key = (grad_products * value_in.astype(jnp.float32)).astype(jnp.bfloat16)
    grad_value = (grad_products * key_in.astype(jnp.float32)).astype(jnp.bfloat16)
    filter_grad = jnp.stack(filter_rows, 0)
    grad_weight, grad_filters = (
        lax.psum_scatter(block_grad, "seq", scatter_dimension=1, tiled=True),
        lax.psum_scatter(filter_grad, "seq", scatter_dimension=1, tiled=True),
    )
    return (grad_query, grad_key, grad_value, grad_weight, grad_filters)


def solution(mesh):
    in_specs = (
        P("seq", "dp"),
        P("seq", "dp"),
        P("seq", "dp"),
        P(None, "dp"),
        P("dp", None),
        P("seq", "dp"),
    )
    out_specs = (P("seq", "dp"), P("seq", "dp"), P("seq", "dp"), P("dp", "seq"), P("dp", "seq"))
    return jax.shard_map(
        per_device, mesh=mesh, in_specs=in_specs, out_specs=out_specs, check_vma=False
    )
```

profile of v0, /device:TPU:8, one launch (start us, length us, event | category | flops | bytes accessed | tf_op | source)
XLA Modules:
  0.0 1246.2 jit_solution(65822679964283518)
XLA Ops:
  8.0 16.3 %all_gather.7 = bf16[16,2048]{1,0:T(8,128)(2,1)S(1)} all-gather(bf16[16,256]{1,0:T(8,128)(2,1)} %param.13), channel_id=1, replica_groups=mesh['seq'=64,'dp'=8] {'dp'}, dimensions={1}, use_global_device_ids=true | all-gather | bytes 73728 | tf_op jit(solution)/shard_map/all_gather | solution.py:60
  26.0 2.6 tile.45
  28.6 4.3 reshape.42
  36.4 4.2 reshape.45
  43.3 4.2 reshape.43
  51.0 4.4 reshape.40
  59.3 104.7 %while.31 = (s32[]{:T(128)}, bf16[256,256]{1,0:T(8,128)(2,1)}, bf16[8,256,256]{2,1,0:T(8,128)(2,1)S(1)}, s32[]{:T(128)}) while((s32[]{:T(128)}, bf16[256,256]{1,0:T(8,128)(2,1)}, bf16[8,256,256]{2,1,0:T(8,128)(2,1)S(1)}, s32[]{:T(128)}) %tuple.66), condition=%wide.region_3.4_spmd, body=%wide.region_2.3_spmd.sunk | while | flops 2 | bytes 1048681 | solution.py:45
  60.7 13.3 %collective-permute-done.1 = bf16[256,256]{1,0:T(8,128)(2,1)S(1)} collective-permute-done((bf16[256,256]{1,0:T(8,128)(2,1)}, bf16[256,256]{1,0:T(8,128)(2,1)S(1)}, u32[]{:S(2)}, u32[]{:S(2)}) %collective-permute-start.1) | collective-permute-done | bytes 131104 | tf_op jit(solution)/shard_map/while/body/eval_jaxpr/ppermute | solution.py:12
  76.0 11.4 collective-permute-done.1
  89.4 10.2 collective-permute-done.1
  101.6 10.6 collective-permute-done.1
  114.2 10.6 collective-permute-done.1
  126.7 10.7 collective-permute-done.1
  139.4 10.7 collective-permute-done.1
  152.1 11.2 collective-permute-done.1
  167.5 98.5 %while.30 = (s32[]{:T(128)}, bf16[256,256]{1,0:T(8,128)(2,1)S(1)}, bf16[8,256,256]{2,1,0:T(8,128)(2,1)S(1)}, s32[]{:T(128)}, s32[]{:T(128)}, /*index=5*/s32[]{:T(128)}, s32[]{:T(128)}) while((s32[]{:T(128)}, bf16[256,256]{1,0:T(8,128)(2,1)S(1)}, bf16[8,256,256]{2,1,0:T(8,128)(2,1)S(1)}, s32[]{:T(128)}, s32[]{:T(128)}, /*index=5*/s32[]{:T(128)}, ...), condition=%wide.region_1.2_spmd, body=%wide.region_0.1_spmd.sunk | while | flops 6 | bytes 1048751 | solution.py:31
  167.5 9.2 collective-permute-start
  179.3 8.3 collective-permute-start
  190.1 8.3 collective-permute-start
  200.9 9.2 collective-permute-start
  210.1 5.0 collective-permute-done
  215.2 8.4 collective-permute-start
  223.6 4.3 collective-permute-done
  228.0 9.4 collective-permute-start
  237.3 3.4 collective-permute-done
  240.8 9.7 collective-permute-start
  250.5 2.8 collective-permute-done
  253.4 10.1 collective-permute-start
  276.2 3.5 reshape.49
  284.5 3.5 reshape.47
  295.6 497.8 %reduce-scatter.7.cloned.1.call-done = f32[32,2]{1,0:T(8,128)} async-done(((f32[2048,2]{1,0:T(8,128)}), f32[32,2]{1,0:T(8,128)}) %reduce-scatter.7.cloned.1.call-update) | async-done | bytes 272
  794.8 444.9 %reduce-scatter.5.cloned.1.call-done = f32[256,32]{0,1:T(8,128)} async-done(((f32[256,2048]{0,1:T(8,128)}), f32[256,32]{0,1:T(8,128)}) %reduce-scatter.5.cloned.1.call-update) | async-done | bytes 32784 | tf_op jit(solution)/shard_map/reduce_scatter | solution.py:109
  (137 shorter events, 69.1 us)
Async XLA Ops:
  7.2 48.3 %copy-start = (bf16[256,2048]{1,0:T(8,128)(2,1)S(1)}, bf16[256,2048]{1,0:T(8,128)(2,1)}, u32[]{:S(2)}) copy-start(bf16[256,2048]{1,0:T(8,128)(2,1)} %param.14) | copy-start | bytes 3145732
  7.2 48.3 %all-gather.2.cloned.1.call-start = ((), (), s32[]{:S(2)}) async-start(), calls=%async_computation.2 | async-start | bytes 1179648 | tf_op jit(solution)/shard_map/all_gather | solution.py:78
  7.9 785.5 %reduce-scatter.7.cloned.1.call-start = ((), (), s32[]{:S(2)}) async-start(), calls=%async_computation.4 | async-start | bytes 1064960
  28.6 4.3 copy-start.18
  43.3 4.2 copy-start.19
  51.0 4.5 copy-start.10
  59.2 104.8 %copy-start.1 = (bf16[256,2559]{1,0:T(8,128)(2,1)S(1)}, bf16[256,2559]{1,0:T(8,128)(2,1)}, u32[]{:S(2)}) copy-start(bf16[256,2559]{1,0:T(8,128)(2,1)} %reshape.45) | copy-start | bytes 3930628
  59.3 14.7 %collective-permute-start.1 = (bf16[256,256]{1,0:T(8,128)(2,1)}, bf16[256,256]{1,0:T(8,128)(2,1)S(1)}, u32[]{:S(2)}, u32[]{:S(2)}) collective-permute-start(bf16[256,256]{1,0:T(8,128)(2,1)} %get-tuple-element.223), channel_id=1, source_target_pairs={{8,0},{16,8},{24,16},{32,24},{40,32},{48,40},{56,48},{64,56},{72,6... | collective-permute-start | bytes 393224 | tf_op jit(solution)/shard_map/while/body/eval_jaxpr/ppermute | solution.py:12
  74.7 12.7 %collective-permute-start.1 = (bf16[256,256]{1,0:T(8,128)(2,1)}, bf16[256,256]{1,0:T(8,128)(2,1)S(1)}, u32[]{:S(2)}, u32[]{:S(2)}) collective-permute-start(bf16[256,256]{1,0:T(8,128)(2,1)} %get-tuple-element.223), channel_id=1, source_target_pairs={{8,0},{16,8},{24,16},{32,24},{40,32},{48,40},{56,48},{64,56},{72,6... | collective-permute-start | bytes 393224 | tf_op jit(solution)/shard_map/while/body/eval_jaxpr/ppermute | solution.py:12
  88.1 11.5 collective-permute-start.1
  100.3 11.9 collective-permute-start.1
  112.9 11.9 collective-permute-start.1
  125.4 12.0 collective-permute-start.1
  138.1 12.0 collective-permute-start.1
  150.8 12.5 %collective-permute-start.1 = (bf16[256,256]{1,0:T(8,128)(2,1)}, bf16[256,256]{1,0:T(8,128)(2,1)S(1)}, u32[]{:S(2)}, u32[]{:S(2)}) collective-permute-start(bf16[256,256]{1,0:T(8,128)(2,1)} %get-tuple-element.223), channel_id=1, source_target_pairs={{8,0},{16,8},{24,16},{32,24},{40,32},{48,40},{56,48},{64,56},{72,6... | collective-permute-start | bytes 393224 | tf_op jit(solution)/shard_map/while/body/eval_jaxpr/ppermute | solution.py:12
  167.5 98.6 %copy-start.5 = (bf16[256,256]{1,0:T(8,128)(2,1)S(1)}, bf16[256,256]{1,0:T(8,128)(2,1)}, u32[]{:S(2)}) copy-start(bf16[256,256]{1,0:T(8,128)(2,1)} %copy-done.3) | copy-start | bytes 393220
  167.5 11.7 collective-permute-start
  179.3 10.8 collective-permute-start
  190.1 10.8 collective-permute-start
  200.9 14.2 %collective-permute-start = (bf16[256,256]{1,0:T(8,128)(2,1)S(1)}, bf16[256,256]{1,0:T(8,128)(2,1)S(1)}, u32[]{:S(2)}, u32[]{:S(2)}) collective-permute-start(bf16[256,256]{1,0:T(8,128)(2,1)S(1)} %get-tuple-element.238), channel_id=1, source_target_pairs={{0,8},{8,16},{16,24},{24,32},{32,40},{40,48},{48,56},{56,64},{64,7... | collective-permute-start | bytes 393224 | tf_op jit(solution)/shard_map/while/body/eval_jaxpr/ppermute | solution.py:12
  215.2 12.7 %collective-permute-start = (bf16[256,256]{1,0:T(8,128)(2,1)S(1)}, bf16[256,256]{1,0:T(8,128)(2,1)S(1)}, u32[]{:S(2)}, u32[]{:S(2)}) collective-permute-start(bf16[256,256]{1,0:T(8,128)(2,1)S(1)} %get-tuple-element.238), channel_id=1, source_target_pairs={{0,8},{8,16},{16,24},{24,32},{32,40},{40,48},{48,56},{56,64},{64,7... | collective-permute-start | bytes 393224 | tf_op jit(solution)/shard_map/while/body/eval_jaxpr/ppermute | solution.py:12
  228.0 12.8 %collective-permute-start = (bf16[256,256]{1,0:T(8,128)(2,1)S(1)}, bf16[256,256]{1,0:T(8,128)(2,1)S(1)}, u32[]{:S(2)}, u32[]{:S(2)}) collective-permute-start(bf16[256,256]{1,0:T(8,128)(2,1)S(1)} %get-tuple-element.238), channel_id=1, source_target_pairs={{0,8},{8,16},{16,24},{24,32},{32,40},{40,48},{48,56},{56,64},{64,7... | collective-permute-start | bytes 393224 | tf_op jit(solution)/shard_map/while/body/eval_jaxpr/ppermute | solution.py:12
  240.8 12.6 %collective-permute-start = (bf16[256,256]{1,0:T(8,128)(2,1)S(1)}, bf16[256,256]{1,0:T(8,128)(2,1)S(1)}, u32[]{:S(2)}, u32[]{:S(2)}) collective-permute-start(bf16[256,256]{1,0:T(8,128)(2,1)S(1)} %get-tuple-element.238), channel_id=1, source_target_pairs={{0,8},{8,16},{16,24},{24,32},{32,40},{40,48},{48,56},{56,64},{64,7... | collective-permute-start | bytes 393224 | tf_op jit(solution)/shard_map/while/body/eval_jaxpr/ppermute | solution.py:12
  253.4 12.6 %collective-permute-start = (bf16[256,256]{1,0:T(8,128)(2,1)S(1)}, bf16[256,256]{1,0:T(8,128)(2,1)S(1)}, u32[]{:S(2)}, u32[]{:S(2)}) collective-permute-start(bf16[256,256]{1,0:T(8,128)(2,1)S(1)} %get-tuple-element.238), channel_id=1, source_target_pairs={{0,8},{8,16},{16,24},{24,32},{32,40},{40,48},{48,56},{56,64},{64,7... | collective-permute-start | bytes 393224 | tf_op jit(solution)/shard_map/while/body/eval_jaxpr/ppermute | solution.py:12
  267.9 1.9 copy-start.6
  288.1 2.4 copy-start.2
  288.1 2.4 copy-start.11
  288.1 2.4 copy-start.12
  288.2 2.4 copy-start.13
  290.5 949.2 %reduce-scatter.5.cloned.1.call-start = ((), (), s32[]{:S(2)}) async-start(), calls=%async_computation.3 | async-start | bytes 2129920 | tf_op jit(solution)/shard_map/reduce_scatter | solution.py:109
  292.5 1.7 copy-start.14
  292.5 2.4 copy-start.9
  (7 other events, 7.8 us)
Sparse Core Ops, SparseCore 0:
  10.0 38.2 all-gather.1
  290.6 502.7 reduce-scatter.6
  796.8 442.8 reduce-scatter.4
where the time goes:
time: 1250 us
  waiting for transfers between devices  1060 us (85%)
  starting transfers between devices  83.1 us (7%)
  local copies, waits for them, and re-layouts  59.8 us (5%)
  blocking collectives  16.3 us (1%)
  between operations  14 us (1%)
    unnamed x4, waiting for transfers between devices  499 us
    reduce_scatter x1, waiting for transfers between devices, per_device(): lax.psum_scatter(block_grad, 'seq', scatter_dimension=1, tiled=True)  445 us
    ppermute x16, waiting for transfers between devices, from_behind(): return lax.ppermute(block, axis, route)  114 us
    ppermute x16, starting transfers between devices, from_behind(): return lax.ppermute(block, axis, route)  83 us
  transfers between devices with their start and end apart: 19, of which 18 were waited for; matrix products, arithmetic and copies ran while one was open for 3% of the time, Pallas kernels for 0%

commit v1 on v0

v1 whole, which is shorter than its diff:
```python
import jax
import jax.numpy as jnp
from jax import lax
from jax.experimental import pallas as pl
from jax.experimental.pallas import tpu as pltpu
from jax.sharding import Mesh
from jax.sharding import PartitionSpec as P

Z, X, H, Y, C = 8, 4, 2, 4, 2
PLANE = ("x", "h")
SEQ = ("z", "x", "h")
BLOCKS = 8
TOK = 256
WIDTH = 256
SLICE = WIDTH // BLOCKS
MODEL = 2048
TAPS = 2048
FILTERS = 16
REACH = TAPS // TOK
SUB = 128
F32, BF16 = jnp.float32, jnp.bfloat16
NN = (((1,), (0,)), ((), ()))
NT = (((1,), (1,)), ((), ()))


def dot(a, b, dims):
    return lax.dot_general(a, b, dims, preferred_element_type=F32)


def flip(a):
    return a.astype(F32).T


def call(body, out_shapes, args, scalars=0, scratch=()):
    specs = [pl.BlockSpec(memory_space=pltpu.SMEM)] * scalars
    specs += [pl.BlockSpec(memory_space=pltpu.VMEM)] * (len(args) - scalars)
    outs = [pl.BlockSpec(memory_space=pltpu.VMEM)] * len(out_shapes)
    return pl.pallas_call(
        body,
        out_shape=[jax.ShapeDtypeStruct(s, t) for s, t in out_shapes],
        in_specs=specs,
        out_specs=outs,
        scratch_shapes=list(scratch),
        name=body.__name__,
    )(*args)


def prepare(q, k, v, gm, filters, pay, p_t, q_t):
    pay[0:WIDTH, :] = flip(gm[...]).astype(BF16)
    pay[WIDTH : WIDTH + FILTERS, :] = filters[...]
    p_t[...] = (k[...].astype(F32) * v[...].astype(F32)).T.astype(BF16)
    q_t[...] = flip(q[...]).astype(BF16)


def project(where, *refs):
    parts = refs[:8]
    weight, q_t, p_t, p_prev, gg_t, send, taps = refs[8:]
    acc = jnp.zeros((WIDTH, TOK), F32)
    rows = lax.broadcasted_iota(jnp.int32, (FILTERS, TOK), 0)
    for n in range(8):
        home = where[n]
        part = parts[n]
        columns = weight[:, pl.ds(pl.multiple_of(home * TOK, TOK), TOK)]
        acc += dot(columns, part[0:WIDTH, :], NN)
        mine = jnp.where(rows == where[8], part[WIDTH : WIDTH + FILTERS, :].astype(F32), 0.0)
        taps[pl.ds(home, 1), :] = jnp.sum(mine, axis=0, keepdims=True)
    gg_t[...] = acc
    gc = (acc * q_t[...].astype(F32)).astype(BF16)
    for r in range(BLOCKS):
        lo, hi = r * SLICE, (r + 1) * SLICE
        send[r, 0:SLICE, :] = p_t[lo:hi, :]
        send[r, SLICE : 2 * SLICE, :] = p_prev[lo:hi, :]
        send[r, 2 * SLICE : 3 * SLICE, :] = gc[lo:hi, :]


def forward(got, taps, band, conv, lags, gc_own, span, folded, sums):
    zero = jnp.zeros((1, SUB), F32)
    pieces = [zero]
    for n in range(TAPS // TOK):
        row = taps[n : n + 1, :]
        pieces += [row[:, 0:SUB], row[:, SUB:TOK]]
    pieces.append(zero)
    blank = jnp.zeros((SUB, SUB), BF16)
    for e in range(-1, 2 * REACH + 2):
        if 0 <= e <= 2 * REACH:
            line = jnp.concatenate([pieces[e], pieces[e + 1]], axis=1)
            wide = jnp.broadcast_to(line, (SUB, 2 * SUB))
            tile = pltpu.roll(wide, 0, 1, stride=1, stride_axis=0)[:, SUB:].astype(BF16)
        else:
            tile = blank
        for d in range(REACH + 1):
            for jb in range(2):
                for ib in range(2):
                    if 2 * d + ib - jb == e:
                        band[d * TOK + jb * SUB : d * TOK + (jb + 1) * SUB, ib * SUB : (ib + 1) * SUB] = tile
    for b in range(BLOCKS):
        span[b * SLICE : (b + 1) * SLICE, :] = got[b, SLICE : 2 * SLICE, :]
        span[WIDTH + b * SLICE : WIDTH + (b + 1) * SLICE, :] = got[b, 0:SLICE, :]
        gc_own[b * SLICE : (b + 1) * SLICE, :] = got[b, 2 * SLICE : 3 * SLICE, :]
    acc = jnp.zeros((WIDTH, TOK), F32)
    for d in range(REACH + 1):
        low = (BLOCKS - d) * SLICE
        acc += dot(span[low : low + WIDTH, :], band[d * TOK : (d + 1) * TOK, :], NN)
    conv[...] = acc.astype(BF16)
    r = lax.broadcasted_iota(jnp.int32, (TOK, TOK), 0)
    c = lax.broadcasted_iota(jnp.int32, (TOK, TOK), 1)
    mirror = jnp.where((r // SUB == c // SUB) & (r % SUB + c % SUB == SUB - 1), 1.0, 0.0).astype(BF16)
    folded[...] = dot(span[...], mirror, NN).astype(BF16)
    grads = flip(gc_own[...]).astype(BF16)
    sums[...] = jnp.zeros(sums.shape, F32)
    for d in range(REACH + 1):
        low = (BLOCKS - d) * SLICE
        m = dot(grads, folded[low : low + WIDTH, :], NN)
        for ib in range(2):
            for jb in range(2):
                e = 2 * d + ib - jb
                if 0 <= e <= 2 * REACH:
                    sums[e] = sums[e] + m[ib * SUB : (ib + 1) * SUB, jb * SUB : (jb + 1) * SUB]
    lines = []
    for e in range(2 * REACH + 1):
        wide = jnp.concatenate([sums[e], jnp.zeros((SUB, SUB), F32)], axis=1)
        lines.append(jnp.sum(pltpu.roll(wide, 1, 1, stride=1, stride_axis=0), axis=0, keepdims=True))
    for e in range(2 * REACH):
        lags[e : e + 1, :] = lines[e][:, SUB:] + lines[e + 1][:, 0:SUB]


def backward(gc_own, gc_next, band, conv, send, span):
    span[0:WIDTH, :] = gc_own[...]
    span[WIDTH : 2 * WIDTH, :] = gc_next[...]
    acc = jnp.zeros((WIDTH, TOK), F32)
    for d in range(REACH + 1):
        acc += dot(span[d * SLICE : d * SLICE + WIDTH, :], band[d * TOK : (d + 1) * TOK, :], NT)
    gp = acc.astype(BF16)
    for b in range(BLOCKS):
        lo, hi = b * SLICE, (b + 1) * SLICE
        send[b, 0:SLICE, :] = conv[lo:hi, :]
        send[b, SLICE : 2 * SLICE, :] = gp[lo:hi, :]


def finish(where, *refs):
    parts = refs[:8]
    got, gg_t, q_t, k, v, lags, gq, gk, gv, send, part_sum = refs[8:]
    conv = jnp.concatenate([got[r, 0:SLICE, :] for r in range(BLOCKS)], axis=0).astype(F32)
    gp = jnp.concatenate([got[r, SLICE : 2 * SLICE, :] for r in range(BLOCKS)], axis=0).astype(F32).T
    gq[...] = (gg_t[...] * conv).T.astype(BF16)
    gk[...] = (gp * v[...].astype(F32)).astype(BF16)
    gv[...] = (gp * k[...].astype(F32)).astype(BF16)
    gated = (q_t[...].astype(F32) * conv).astype(BF16)
    per = TOK // 32
    for n in range(8):
        part_sum[...] = dot(parts[n][0:WIDTH, :], gated, NT).astype(BF16)
        home = where[n]
        for s in range(per):
            send[home * per + s, 0:32, :] = part_sum[s * 32 : (s + 1) * 32, :]
    rows = lax.broadcasted_iota(jnp.int32, (8, WIDTH), 0)
    mine = where[9]
    for e in range(16):
        line = lags[e : e + 1, :]
        for s in range(4):
            cut = line[:, s * 32 : (s + 1) * 32]
            wide = jnp.concatenate([cut, jnp.zeros((1, WIDTH - 32), F32)], axis=1)
            top = wide.astype(BF16)
            low = wide - top.astype(F32)
            tile = jnp.where(rows == mine, top.astype(F32), jnp.where(rows == mine + 2, low, 0.0))
            send[e * 4 + s, 32:40, :] = tile.astype(BF16)


def collect(got, gw, gf):
    acc = jnp.zeros((40, WIDTH), F32)
    for s in range(64):
        acc += got[s].astype(F32)
    gw[...] = acc[0:32, :].T
    gf[...] = acc[32:34, 0:32] + acc[34:36, 0:32]


def shift(block, axis, distance, size):
    return lax.ppermute(block, axis, [(i, i + distance) for i in range(size) if 0 <= i + distance < size])


def per_device(q, k, v, filters, weight, gm):
    y, c = lax.axis_index("y"), lax.axis_index("c")
    own_filter = lax.axis_index("x") // 2
    pay, p_t, q_t = call(
        prepare, [((WIDTH + FILTERS, TOK), BF16), ((WIDTH, TOK), BF16), ((WIDTH, TOK), BF16)], (q, k, v, gm, filters)
    )
    line = [pay] + [lax.ppermute(pay, "y", [(i, (i + n) % Y) for i in range(Y)]) for n in range(1, Y)]
    other = [lax.ppermute(part, "c", [(0, 1), (1, 0)]) for part in line]
    parts = line + other
    homes = [((y - n) % Y) * C + c for n in range(Y)] + [((y - n) % Y) * C + 1 - c for n in range(Y)]
    where = jnp.stack(homes + [(y * C + c) * 2 + own_filter, own_filter]).astype(jnp.int32)
    p_prev = shift(p_t, "z", 1, Z)
    gg_t, send, taps = call(
        project,
        [((WIDTH, TOK), F32), ((BLOCKS, 3 * SLICE, TOK), BF16), ((TAPS // TOK, TOK), F32)],
        (where, *parts, weight, q_t, p_t, p_prev),
        scalars=1,
    )
    got = lax.all_to_all(send, PLANE, 0, 0, tiled=True)
    gc_early = got[:, 2 * SLICE :, :].reshape(WIDTH, TOK)
    gc_next = shift(gc_early, "z", -1, Z)
    band, conv, lags, gc_own = call(
        forward,
        [(((REACH + 1) * TOK, TOK), BF16), ((WIDTH, TOK), BF16), ((16, SUB), F32), ((WIDTH, TOK), BF16)],
        (got, taps),
        scratch=(
            pltpu.VMEM((2 * WIDTH, TOK), BF16),
            pltpu.VMEM((2 * WIDTH, TOK), BF16),
            pltpu.VMEM((2 * REACH + 1, SUB, SUB), F32),
        ),
    )
    (send,) = call(
        backward,
        [((BLOCKS, 2 * SLICE, TOK), BF16)],
        (gc_own, gc_next, band, conv),
        scratch=(pltpu.VMEM((2 * WIDTH, TOK), BF16),),
    )
    got = lax.all_to_all(send, PLANE, 0, 0, tiled=True)
    gq, gk, gv, send = call(
        finish,
        [((TOK, WIDTH), BF16)] * 3 + [((64, 40, WIDTH), BF16)],
        (where, *parts, got, gg_t, q_t, k, v, lags),
        scalars=1,
        scratch=(pltpu.VMEM((TOK, WIDTH), BF16),),
    )
    got = lax.all_to_all(send, SEQ, 0, 0, tiled=True)
    gw, gf = call(collect, [((WIDTH, 32), F32), ((2, 32), F32)], (got,))
    return gq, gk, gv, gw, gf


def solution(mesh):
    fine = Mesh(mesh.devices.reshape(Z, X, H, Y, C), ("z", "x", "h", "y", "c"))
    seq, dp = SEQ, ("y", "c")
    in_specs = (P(seq, dp), P(seq, dp), P(seq, dp), P(None, dp), P(dp, None), P(seq, dp))
    out_specs = (P(seq, dp), P(seq, dp), P(seq, dp), P(dp, seq), P(dp, seq))
    return jax.shard_map(per_device, mesh=fine, in_specs=in_specs, out_specs=out_specs, check_vma=False)
```

time: 1250 us -> 140 us (0.11)
  waiting for transfers between devices: 1060 us -> 5.78 us
  blocking collectives: 16.3 us -> 87.7 us
  starting transfers between devices: 83.1 us -> 25.5 us
  local copies, waits for them, and re-layouts: 59.8 us -> 3.63 us
  Pallas kernels: 0 us -> 15.7 us
  between operations: 14 us -> 0.92 us
    unnamed x4 -> x0, waiting for transfers between devices: 499 us -> none
    reduce_scatter x1 -> x0, waiting for transfers between devices: 445 us -> none  [per_device(): lax.psum_scatter(block_grad, 'seq', scatter_dimension=1, tiled=True)]
    ppermute x16 -> x9, waiting for transfers between devices: 114 us -> 5.78 us  [the longest x2 5.76 us: shift(): lax.ppermute(block, axis, [(i, i + distance) for i in range(size) if 0 <=...]
    all_to_all x0 -> x3, blocking collectives: none -> 87.7 us  [the longest x1 45.9 us: per_device(): got = lax.all_to_all(send, SEQ, 0, 0, tiled=True)]
    ppermute x16 -> x9, starting transfers between devices: 83 us -> 25.5 us  [the longest x3 13.9 us: per_device(): lax.ppermute(pay, 'y', [(i, (i + n) % Y) for i in range(Y)])]
    reshape x8 -> x0, local copies, waits for them, and re-layouts: 28.8 us -> none  [the longest x4 17.2 us: band_matrix(): return tiled.reshape(row_count, period - 1)[:, :col_count]]
    all_gather x1 -> x0, blocking collectives: 16.3 us -> none  [per_device(): all_taps = lax.all_gather(filters, 'dp', axis=1, tiled=True)]
    pallas_call x0 -> x6, Pallas kernels: none -> 15.7 us  [call(): pl.pallas_call(body, out_shape=[jax.ShapeDtypeStruct(s, t) for s, t in ou...]
  transfers between devices with their start and end apart: 19 -> 9, of which waited for: 18 -> 2; matrix products, arithmetic and copies ran while one was open for 3% -> 0% of each run, Pallas kernels for 0% -> 2%
where the time goes in v1:
time: 140 us; the launch traced here: 139 us
  blocking collectives  87.7 us (63%)
  starting transfers between devices  25.5 us (18%)
  Pallas kernels  15.7 us (11%)
  waiting for transfers between devices  5.78 us (4%)
  local copies, waits for them, and re-layouts  3.63 us (3%)
    all_to_all x1, blocking collectives, per_device(): got = lax.all_to_all(send, SEQ, 0, 0, tiled=True)  45.9 us
    all_to_all x2, blocking collectives, per_device(): got = lax.all_to_all(send, PLANE, 0, 0, tiled=True)  41.8 us
    pallas_call x6, Pallas kernels, call(): pl.pallas_call(body, out_shape=[jax.ShapeDtypeStruct(s, t) for s, t in ou...  15.7 us
    ppermute x3, starting transfers between devices, per_device(): lax.ppermute(pay, 'y', [(i, (i + n) % Y) for i in range(Y)])  13.9 us
    ppermute x4, starting transfers between devices, per_device(): other = [lax.ppermute(part, 'c', [(0, 1), (1, 0)]) for part in line]  8.65 us
    ppermute x2, waiting for transfers between devices, shift(): lax.ppermute(block, axis, [(i, i + distance) for i in range(size) if 0 <=...  5.76 us
    unnamed x21, local copies, waits for them, and re-layouts  3.01 us
    ppermute x2, starting transfers between devices, shift(): lax.ppermute(block, axis, [(i, i + distance) for i in range(size) if 0 <=...  2.98 us
  transfers between devices with their start and end apart: 9, of which 2 were waited for; matrix products, arithmetic and copies ran while one was open for 0% of the time, Pallas kernels for 2%

profile of v1, /device:TPU:8, one launch (start us, length us, event | category | flops | bytes accessed | tf_op | source)
XLA Modules:
  0.0 139.2 jit_solution(2383079841598704497)
XLA Ops:
  0.6 1.9 %prepare.1 = (bf16[272,256]{1,0:T(8,128)(2,1)}, bf16[256,256]{1,0:T(8,128)(2,1)}, bf16[256,256]{1,0:T(8,128)(2,1)}) custom-call(bf16[256,256]{1,0:T(8,128)(2,1)} %q.1, bf16[256,256]{1,0:T(8,128)(2,1)} %refs_11_.1, bf16[256,256]{1,0:T(8,128)(2,1)} %refs_12_.1, bf16[256,256]{1,0:T(8,128)(2,1)} %gm.1, bf16[16,256]{1,0:T(8,128)(2,1)} %filters.1), custom_call_target="tpu_custom_call" | custom-call | tf_op jit(solution)/shard_map/prepare/pallas_call | solution.py:38
  2.6 3.5 %collective-permute-start = (bf16[272,256]{1,0:T(8,128)(2,1)}, bf16[272,256]{1,0:T(8,128)(2,1)S(1)}, u32[]{:S(2)}, u32[]{:S(2)}) collective-permute-start(bf16[272,256]{1,0:T(8,128)(2,1)} %get-tuple-element.21.refs_0_), channel_id=1, source_target_pairs={{0,2},{2,4},{4,6},{6,0},{1,3},{3,5},{5,7},{7,1},{8,10},{10,12},{12... | collective-permute-start | bytes 417800 | tf_op jit(solution)/shard_map/ppermute | solution.py:186
  6.0 8.5 %collective-permute-start.1 = (bf16[272,256]{1,0:T(8,128)(2,1)}, bf16[272,256]{1,0:T(8,128)(2,1)S(1)}, u32[]{:S(2)}, u32[]{:S(2)}) collective-permute-start(bf16[272,256]{1,0:T(8,128)(2,1)} %get-tuple-element.21.refs_0_), channel_id=1, source_target_pairs={{0,4},{2,6},{4,0},{6,2},{1,5},{3,7},{5,1},{7,3},{8,12},{10,14},{12... | collective-permute-start | bytes 417800 | tf_op jit(solution)/shard_map/ppermute | solution.py:186
  14.5 1.9 %collective-permute-start.2 = (bf16[272,256]{1,0:T(8,128)(2,1)}, bf16[272,256]{1,0:T(8,128)(2,1)S(1)}, u32[]{:S(2)}, u32[]{:S(2)}) collective-permute-start(bf16[272,256]{1,0:T(8,128)(2,1)} %get-tuple-element.21.refs_0_), channel_id=1, source_target_pairs={{0,6},{2,0},{4,2},{6,4},{1,7},{3,1},{5,3},{7,5},{8,14},{10,8},{12,... | collective-permute-start | bytes 417800 | tf_op jit(solution)/shard_map/ppermute | solution.py:186
  16.5 1.9 %collective-permute-start.3 = (bf16[272,256]{1,0:T(8,128)(2,1)}, bf16[272,256]{1,0:T(8,128)(2,1)S(1)}, u32[]{:S(2)}, u32[]{:S(2)}) collective-permute-start(bf16[272,256]{1,0:T(8,128)(2,1)} %get-tuple-element.21.refs_0_), channel_id=1, source_target_pairs={{0,1},{1,0},{2,3},{3,2},{4,5},{5,4},{6,7},{7,6},{8,9},{9,8},{10,11... | collective-permute-start | bytes 417800 | tf_op jit(solution)/shard_map/ppermute | solution.py:187
  18.4 0.0 collective-permute-done.refs_1_
  18.4 2.4 %collective-permute-start.4 = (bf16[272,256]{1,0:T(8,128)(2,1)S(1)}, bf16[272,256]{1,0:T(8,128)(2,1)S(1)}, u32[]{:S(2)}, u32[]{:S(2)}) collective-permute-start(bf16[272,256]{1,0:T(8,128)(2,1)S(1)} %collective-permute-done.refs_1_), channel_id=1, source_target_pairs={{0,1},{1,0},{2,3},{3,2},{4,5},{5,4},{6,7},{7,6},{8,9},{9,8},{10,11... | collective-permute-start | bytes 417800 | tf_op jit(solution)/shard_map/ppermute | solution.py:187
  20.8 1.9 %collective-permute-start.5 = (bf16[272,256]{1,0:T(8,128)(2,1)S(1)}, bf16[272,256]{1,0:T(8,128)(2,1)S(1)}, u32[]{:S(2)}, u32[]{:S(2)}) collective-permute-start(bf16[272,256]{1,0:T(8,128)(2,1)S(1)} %collective-permute-done.1.refs_2_), channel_id=1, source_target_pairs={{0,1},{1,0},{2,3},{3,2},{4,5},{5,4},{6,7},{7,6},{8,9},{9,8},{10,11... | collective-permute-start | bytes 417800 | tf_op jit(solution)/shard_map/ppermute | solution.py:187
  22.8 0.0 collective-permute-done.2.refs_3_
  22.8 2.4 %collective-permute-start.6 = (bf16[272,256]{1,0:T(8,128)(2,1)S(1)}, bf16[272,256]{1,0:T(8,128)(2,1)S(1)}, u32[]{:S(2)}, u32[]{:S(2)}) collective-permute-start(bf16[272,256]{1,0:T(8,128)(2,1)S(1)} %collective-permute-done.2.refs_3_), channel_id=1, source_target_pairs={{0,1},{1,0},{2,3},{3,2},{4,5},{5,4},{6,7},{7,6},{8,9},{9,8},{10,11... | collective-permute-start | bytes 417800 | tf_op jit(solution)/shard_map/ppermute | solution.py:187
  25.2 1.7 %collective-permute-start.7 = (bf16[256,256]{1,0:T(8,128)(2,1)}, bf16[256,256]{1,0:T(8,128)(2,1)S(1)}, u32[]{:S(2)}, u32[]{:S(2)}) collective-permute-start(bf16[256,256]{1,0:T(8,128)(2,1)} %get-tuple-element.23.refs_10_), channel_id=1, source_target_pairs={{0,64},{64,128},{128,192},{192,256},{256,320},{320,384},{384,448},... | collective-permute-start | bytes 393224 | tf_op jit(solution)/shard_map/ppermute | solution.py:177
  27.0 0.6 stack.43.where
  27.6 2.5 %collective-permute-done.7.refs_11_ = bf16[256,256]{1,0:T(8,128)(2,1)S(1)} collective-permute-done((bf16[256,256]{1,0:T(8,128)(2,1)}, bf16[256,256]{1,0:T(8,128)(2,1)S(1)}, u32[]{:S(2)}, u32[]{:S(2)}) %collective-permute-start.7) | collective-permute-done | bytes 131104 | tf_op jit(solution)/shard_map/ppermute | solution.py:177
  30.1 0.0 collective-permute-done.3.refs_4_
  30.1 0.0 collective-permute-done.4.refs_5_
  30.2 0.6 copy-done.9
  30.8 0.1 copy-done.4
  30.8 0.0 copy-done.5
  30.9 0.0 copy-done.6
  30.9 0.0 copy-done.7
  31.0 3.1 %project.1 = (f32[256,256]{1,0:T(8,128)}, bf16[8,96,256]{2,1,0:T(8,128)(2,1)}, f32[8,256]{1,0:T(8,128)}) custom-call(s32[10]{0:T(128)} %stack.43.where, bf16[272,256]{1,0:T(8,128)(2,1)} %get-tuple-element.21.refs_0_, bf16[272,256]{1,0:T(8,128)(2,1)} %copy-done.1, bf16[272,256]{1,0:T(8,128)(2,1)} %copy-done.2, bf16[272,256]{1,0:T(8,128)(2,1)} %copy-done.3, ...), custom_call_target="tpu_custom_call" | custom-call | tf_op jit(solution)/shard_map/project/pallas_call | solution.py:38
  34.0 25.9 %all_to_all.15.got = bf16[8,96,256]{2,1,0:T(8,128)(2,1)S(1)} all-to-all(bf16[8,96,256]{2,1,0:T(8,128)(2,1)} %get-tuple-element.24), channel_id=1, replica_groups=mesh['z'=8,'x'=4,'h'=2,'y'=4,'c'=2] {'x','h'}, dimensions={0} | all-to-all | bytes 786432 | tf_op jit(solution)/shard_map/all_to_all | solution.py:198
  59.9 1.3 collective-permute-start.8
  61.2 2.7 %forward.1 = (bf16[2304,256]{1,0:T(8,128)(2,1)}, bf16[256,256]{1,0:T(8,128)(2,1)}, f32[16,128]{1,0:T(8,128)}, bf16[256,256]{1,0:T(8,128)(2,1)}) custom-call(bf16[8,96,256]{2,1,0:T(8,128)(2,1)} %copy-done, f32[8,256]{1,0:T(8,128)} %get-tuple-element.25.taps), custom_call_target="tpu_custom_call" | custom-call | tf_op jit(solution)/shard_map/forward/pallas_call | solution.py:38
  63.9 3.2 %collective-permute-done.8.gc_next = bf16[256,256]{1,0:T(8,128)(2,1)S(1)} collective-permute-done((bf16[256,256]{1,0:T(8,128)(2,1)S(1)}, bf16[256,256]{1,0:T(8,128)(2,1)S(1)}, u32[]{:S(2)}, u32[]{:S(2)}) %collective-permute-start.8) | collective-permute-done | bytes 131104 | tf_op jit(solution)/shard_map/ppermute | solution.py:177
  67.2 0.7 copy-done.8
  67.8 2.6 %backward.1 = bf16[8,64,256]{2,1,0:T(8,128)(2,1)} custom-call(bf16[256,256]{1,0:T(8,128)(2,1)} %get-tuple-element.26.gc_own, bf16[256,256]{1,0:T(8,128)(2,1)} %copy-done.8, bf16[2304,256]{1,0:T(8,128)(2,1)} %get-tuple-element.27.band, bf16[256,256]{1,0:T(8,128)(2,1)} %get-tuple-element.28.conv), custom_call_target="tpu_custom_call" | custom-call | tf_op jit(solution)/shard_map/backward/pallas_call | solution.py:38
  70.4 15.9 %all_to_all.16.refs_8_ = bf16[8,64,256]{2,1,0:T(8,128)(2,1)} all-to-all(bf16[8,64,256]{2,1,0:T(8,128)(2,1)} %backward.1), channel_id=1, replica_groups=mesh['z'=8,'x'=4,'h'=2,'y'=4,'c'=2] {'x','h'}, dimensions={0} | all-to-all | bytes 524288 | tf_op jit(solution)/shard_map/all_to_all | solution.py:217
  86.3 3.2 %finish.1 = (bf16[256,256]{1,0:T(8,128)(2,1)}, bf16[256,256]{1,0:T(8,128)(2,1)}, bf16[256,256]{1,0:T(8,128)(2,1)}, bf16[64,40,256]{2,1,0:T(8,128)(2,1)}) custom-call(s32[10]{0:T(128)} %stack.43.where, bf16[272,256]{1,0:T(8,128)(2,1)} %get-tuple-element.21.refs_0_, bf16[272,256]{1,0:T(8,128)(2,1)} %copy-done.1, bf16[272,256]{1,0:T(8,128)(2,1)} %copy-done.2, ...), custom_call_target="tpu_custom_call" | custom-call | tf_op jit(solution)/shard_map/finish/pallas_call | solution.py:38
  89.5 45.9 %all_to_all.17.got = bf16[64,40,256]{2,1,0:T(8,128)(2,1)} all-to-all(bf16[64,40,256]{2,1,0:T(8,128)(2,1)} %get-tuple-element.34), channel_id=1, replica_groups=mesh['z'=8,'x'=4,'h'=2,'y'=4,'c'=2] {'z','x','h'}, dimensions={0} | all-to-all | bytes 2621440 | tf_op jit(solution)/shard_map/all_to_all | solution.py:225
  135.4 2.2 %collect.1 = (f32[256,32]{1,0:T(8,128)}, f32[2,32]{1,0:T(2,128)}) custom-call(bf16[64,40,256]{2,1,0:T(8,128)(2,1)} %all_to_all.17.got), custom_call_target="tpu_custom_call" | custom-call | tf_op jit(solution)/shard_map/collect/pallas_call | solution.py:38
  137.6 1.6 %copy.11 = f32[256,32]{0,1:T(8,128)} copy(f32[256,32]{1,0:T(8,128)} %get-tuple-element.40) | data formatting | bytes 65536
  (18 shorter events, 0.0 us)
Async XLA Ops:
  2.6 15.8 %collective-permute-start = (bf16[272,256]{1,0:T(8,128)(2,1)}, bf16[272,256]{1,0:T(8,128)(2,1)S(1)}, u32[]{:S(2)}, u32[]{:S(2)}) collective-permute-start(bf16[272,256]{1,0:T(8,128)(2,1)} %get-tuple-element.21.refs_0_), channel_id=1, source_target_pairs={{0,2},{2,4},{4,6},{6,0},{1,3},{3,5},{5,7},{7,1},{8,10},{10,12},{12... | collective-permute-start | bytes 417800 | tf_op jit(solution)/shard_map/ppermute | solution.py:186
  6.0 14.8 %collective-permute-start.1 = (bf16[272,256]{1,0:T(8,128)(2,1)}, bf16[272,256]{1,0:T(8,128)(2,1)S(1)}, u32[]{:S(2)}, u32[]{:S(2)}) collective-permute-start(bf16[272,256]{1,0:T(8,128)(2,1)} %get-tuple-element.21.refs_0_), channel_id=1, source_target_pairs={{0,4},{2,6},{4,0},{6,2},{1,5},{3,7},{5,1},{7,3},{8,12},{10,14},{12... | collective-permute-start | bytes 417800 | tf_op jit(solution)/shard_map/ppermute | solution.py:186
  14.5 8.2 %collective-permute-start.2 = (bf16[272,256]{1,0:T(8,128)(2,1)}, bf16[272,256]{1,0:T(8,128)(2,1)S(1)}, u32[]{:S(2)}, u32[]{:S(2)}) collective-permute-start(bf16[272,256]{1,0:T(8,128)(2,1)} %get-tuple-element.21.refs_0_), channel_id=1, source_target_pairs={{0,6},{2,0},{4,2},{6,4},{1,7},{3,1},{5,3},{7,5},{8,14},{10,8},{12,... | collective-permute-start | bytes 417800 | tf_op jit(solution)/shard_map/ppermute | solution.py:186
  16.5 13.7 %collective-permute-start.3 = (bf16[272,256]{1,0:T(8,128)(2,1)}, bf16[272,256]{1,0:T(8,128)(2,1)S(1)}, u32[]{:S(2)}, u32[]{:S(2)}) collective-permute-start(bf16[272,256]{1,0:T(8,128)(2,1)} %get-tuple-element.21.refs_0_), channel_id=1, source_target_pairs={{0,1},{1,0},{2,3},{3,2},{4,5},{5,4},{6,7},{7,6},{8,9},{9,8},{10,11... | collective-permute-start | bytes 417800 | tf_op jit(solution)/shard_map/ppermute | solution.py:187
  18.4 11.8 %copy-start.1 = (bf16[272,256]{1,0:T(8,128)(2,1)}, bf16[272,256]{1,0:T(8,128)(2,1)S(1)}, u32[]{:S(2)}) copy-start(bf16[272,256]{1,0:T(8,128)(2,1)S(1)} %collective-permute-done.refs_1_) | copy-start | bytes 417796
  18.4 11.7 %collective-permute-start.4 = (bf16[272,256]{1,0:T(8,128)(2,1)S(1)}, bf16[272,256]{1,0:T(8,128)(2,1)S(1)}, u32[]{:S(2)}, u32[]{:S(2)}) collective-permute-start(bf16[272,256]{1,0:T(8,128)(2,1)S(1)} %collective-permute-done.refs_1_), channel_id=1, source_target_pairs={{0,1},{1,0},{2,3},{3,2},{4,5},{5,4},{6,7},{7,6},{8,9},{9,8},{10,11... | collective-permute-start | bytes 417800 | tf_op jit(solution)/shard_map/ppermute | solution.py:187
  20.8 9.4 %copy-start.2 = (bf16[272,256]{1,0:T(8,128)(2,1)}, bf16[272,256]{1,0:T(8,128)(2,1)S(1)}, u32[]{:S(2)}) copy-start(bf16[272,256]{1,0:T(8,128)(2,1)S(1)} %collective-permute-done.1.refs_2_) | copy-start | bytes 417796
  20.8 9.3 %collective-permute-start.5 = (bf16[272,256]{1,0:T(8,128)(2,1)S(1)}, bf16[272,256]{1,0:T(8,128)(2,1)S(1)}, u32[]{:S(2)}, u32[]{:S(2)}) collective-permute-start(bf16[272,256]{1,0:T(8,128)(2,1)S(1)} %collective-permute-done.1.refs_2_), channel_id=1, source_target_pairs={{0,1},{1,0},{2,3},{3,2},{4,5},{5,4},{6,7},{7,6},{8,9},{9,8},{10,11... | collective-permute-start | bytes 417800 | tf_op jit(solution)/shard_map/ppermute | solution.py:187
  22.8 7.4 %copy-start.3 = (bf16[272,256]{1,0:T(8,128)(2,1)}, bf16[272,256]{1,0:T(8,128)(2,1)S(1)}, u32[]{:S(2)}) copy-start(bf16[272,256]{1,0:T(8,128)(2,1)S(1)} %collective-permute-done.2.refs_3_) | copy-start | bytes 417796
  22.8 7.4 %collective-permute-start.6 = (bf16[272,256]{1,0:T(8,128)(2,1)S(1)}, bf16[272,256]{1,0:T(8,128)(2,1)S(1)}, u32[]{:S(2)}, u32[]{:S(2)}) collective-permute-start(bf16[272,256]{1,0:T(8,128)(2,1)S(1)} %collective-permute-done.2.refs_3_), channel_id=1, source_target_pairs={{0,1},{1,0},{2,3},{3,2},{4,5},{5,4},{6,7},{7,6},{8,9},{9,8},{10,11... | collective-permute-start | bytes 417800 | tf_op jit(solution)/shard_map/ppermute | solution.py:187
  25.2 4.9 %collective-permute-start.7 = (bf16[256,256]{1,0:T(8,128)(2,1)}, bf16[256,256]{1,0:T(8,128)(2,1)S(1)}, u32[]{:S(2)}, u32[]{:S(2)}) collective-permute-start(bf16[256,256]{1,0:T(8,128)(2,1)} %get-tuple-element.23.refs_10_), channel_id=1, source_target_pairs={{0,64},{64,128},{128,192},{192,256},{256,320},{320,384},{384,448},... | collective-permute-start | bytes 393224 | tf_op jit(solution)/shard_map/ppermute | solution.py:177
  30.1 0.7 copy-start.9
  30.1 0.7 copy-start.4
  30.1 0.7 copy-start.5
  30.2 0.8 copy-start.6
  30.2 0.8 copy-start.7
  59.9 1.3 copy-start
  59.9 7.2 %collective-permute-start.8 = (bf16[256,256]{1,0:T(8,128)(2,1)S(1)}, bf16[256,256]{1,0:T(8,128)(2,1)S(1)}, u32[]{:S(2)}, u32[]{:S(2)}) collective-permute-start(bf16[256,256]{1,0:T(8,128)(2,1)S(1)} %bitcast.11), channel_id=1, source_target_pairs={{64,0},{128,64},{192,128},{256,192},{320,256},{384,320},{448,384},... | collective-permute-start | bytes 393224 | tf_op jit(solution)/shard_map/ppermute | solution.py:177
  67.2 0.7 copy-start.8

commit v2 on v1

v2 whole, which is shorter than its diff:
```python
import jax
import jax.numpy as jnp
from jax import lax
from jax.experimental import pallas as pl
from jax.experimental.pallas import tpu as pltpu
from jax.sharding import Mesh
from jax.sharding import PartitionSpec as P

Z, X, H, Y, C = 8, 4, 2, 4, 2
PLANE = ("x", "h")
SEQ = ("z", "x", "h")
BLOCKS = 8
TOK = 256
WIDTH = 256
SLICE = WIDTH // BLOCKS
MODEL = 2048
TAPS = 2048
FILTERS = 16
REACH = TAPS // TOK
SUB = 128
PAY = WIDTH + FILTERS
ROWS = SLICE + 8
F32, BF16 = jnp.float32, jnp.bfloat16
NN = (((1,), (0,)), ((), ()))
NT = (((1,), (1,)), ((), ()))


def dot(a, b, dims):
    return lax.dot_general(a, b, dims, preferred_element_type=F32)


def flip(a):
    return a.astype(F32).T


def call(body, out_shapes, args, scalars=0, scratch=()):
    specs = [pl.BlockSpec(memory_space=pltpu.SMEM)] * scalars
    specs += [pl.BlockSpec(memory_space=pltpu.VMEM)] * (len(args) - scalars)
    outs = [pl.BlockSpec(memory_space=pltpu.VMEM)] * len(out_shapes)
    return pl.pallas_call(
        body,
        out_shape=[jax.ShapeDtypeStruct(s, t) for s, t in out_shapes],
        in_specs=specs,
        out_specs=outs,
        scratch_shapes=list(scratch),
        name=body.__name__,
    )(*args)


def prepare(q, k, v, gm, filters, pay, p_t, q_t):
    pay[0:WIDTH, :] = flip(gm[...]).astype(BF16)
    pay[WIDTH:PAY, :] = filters[...]
    p_t[...] = (k[...].astype(F32) * v[...].astype(F32)).T.astype(BF16)
    q_t[...] = flip(q[...]).astype(BF16)


def fill_band(band, taps):
    zero = jnp.zeros((1, SUB), F32)
    pieces = [zero]
    for n in range(TAPS // TOK):
        row = taps[n : n + 1, :]
        pieces += [row[:, 0:SUB], row[:, SUB:TOK]]
    pieces.append(zero)
    for e in range(-1, 2 * REACH + 2):
        if 0 <= e <= 2 * REACH:
            line = jnp.concatenate([pieces[e], pieces[e + 1]], axis=1)
            wide = jnp.broadcast_to(line, (SUB, 2 * SUB))
            tile = pltpu.roll(wide, 0, 1, stride=1, stride_axis=0)[:, SUB:].astype(BF16)
        else:
            tile = jnp.zeros((SUB, SUB), BF16)
        for d in range(REACH + 1):
            for jb in range(2):
                for ib in range(2):
                    if 2 * d + ib - jb == e:
                        band[d * TOK + jb * SUB : d * TOK + (jb + 1) * SUB, ib * SUB : (ib + 1) * SUB] = tile


def project(where, own, other, weight, q_t, p_got, p_prev, gg_t, send, band, taps, span):
    acc = jnp.zeros((WIDTH, TOK), F32)
    rows = lax.broadcasted_iota(jnp.int32, (FILTERS, TOK), 0)
    for n in range(8):
        home = where[n]
        part, low = (own, n * PAY) if n < Y else (other, (n - Y) * PAY)
        columns = weight[:, pl.ds(pl.multiple_of(home * TOK, TOK), TOK)]
        acc += dot(columns, part[low : low + WIDTH, :], NN)
        mine = jnp.where(rows == where[8], part[low + WIDTH : low + PAY, :].astype(F32), 0.0)
        taps[pl.ds(home, 1), :] = jnp.sum(mine, axis=0, keepdims=True)
    gg_t[...] = acc
    gc = (acc * q_t[...].astype(F32)).astype(BF16)
    fill_band(band, taps)
    span[0:WIDTH, :] = p_prev[...]
    for b in range(BLOCKS):
        span[WIDTH + b * SLICE : WIDTH + (b + 1) * SLICE, :] = p_got[b]
    acc = jnp.zeros((WIDTH, TOK), F32)
    for d in range(REACH + 1):
        low = (BLOCKS - d) * SLICE
        acc += dot(span[low : low + WIDTH, :], band[d * TOK : (d + 1) * TOK, :], NN)
    conv = acc.astype(BF16)
    for r in range(BLOCKS):
        lo, hi = r * SLICE, (r + 1) * SLICE
        send[r, 0:SLICE, :] = conv[lo:hi, :]
        send[r, SLICE : 2 * SLICE, :] = gc[lo:hi, :]


def conv_of(got):
    return jnp.concatenate([got[r, 0:SLICE, :] for r in range(BLOCKS)], axis=0).astype(F32)


def weigh(where, own, other, got, q_t, send, part_sum):
    gated = (q_t[...].astype(F32) * conv_of(got)).astype(BF16)
    for n in range(8):
        part, low = (own, n * PAY) if n < Y else (other, (n - Y) * PAY)
        part_sum[...] = dot(part[low : low + WIDTH, :], gated, NT).astype(BF16)
        at = pl.multiple_of(where[n] * SLICE, SLICE)
        for x in range(X):
            for h in range(H):
                lo = (x * H + h) * SLICE
                send[x, pl.ds(h * WIDTH + at, SLICE), :] = part_sum[lo : lo + SLICE, :]


def backward(got, gc_next, band, p_got, p_prev, gg_t, send, gq, ahead, span, folded, sums):
    gq[...] = (gg_t[...] * conv_of(got)).T.astype(BF16)
    span[0:WIDTH, :] = p_prev[...]
    for b in range(BLOCKS):
        span[WIDTH + b * SLICE : WIDTH + (b + 1) * SLICE, :] = p_got[b]
        ahead[b * SLICE : (b + 1) * SLICE, :] = got[b, SLICE : 2 * SLICE, :]
    ahead[WIDTH : 2 * WIDTH, :] = gc_next[...]
    acc = jnp.zeros((WIDTH, TOK), F32)
    for d in range(REACH + 1):
        acc += dot(ahead[d * SLICE : d * SLICE + WIDTH, :], band[d * TOK : (d + 1) * TOK, :], NT)
    gp = acc.astype(BF16)
    for b in range(BLOCKS):
        send[b, 0:SLICE, :] = gp[b * SLICE : (b + 1) * SLICE, :]
    r = lax.broadcasted_iota(jnp.int32, (TOK, TOK), 0)
    c = lax.broadcasted_iota(jnp.int32, (TOK, TOK), 1)
    mirror = jnp.where((r // SUB == c // SUB) & (r % SUB + c % SUB == SUB - 1), 1.0, 0.0).astype(BF16)
    folded[...] = dot(span[...], mirror, NN).astype(BF16)
    grads = flip(ahead[0:WIDTH, :]).astype(BF16)
    sums[...] = jnp.zeros(sums.shape, F32)
    for d in range(REACH + 1):
        low = (BLOCKS - d) * SLICE
        m = dot(grads, folded[low : low + WIDTH, :], NN)
        for ib in range(2):
            for jb in range(2):
                e = 2 * d + ib - jb
                if 0 <= e <= 2 * REACH:
                    sums[e] = sums[e] + m[ib * SUB : (ib + 1) * SUB, jb * SUB : (jb + 1) * SUB]
    lines = []
    for e in range(2 * REACH + 1):
        wide = jnp.concatenate([sums[e], jnp.zeros((SUB, SUB), F32)], axis=1)
        lines.append(jnp.sum(pltpu.roll(wide, 1, 1, stride=1, stride_axis=0), axis=0, keepdims=True))
    for odd in range(2):
        lags = [lines[e][:, SUB:] + lines[e + 1][:, 0:SUB] for e in range(odd, 2 * REACH, 2)]
        both = split(jnp.concatenate(lags, axis=0))
        for b in range(BLOCKS // 2):
            send[odd * (BLOCKS // 2) + b, SLICE:ROWS, :] = both


def split(a):
    high = a.astype(BF16)
    return jnp.concatenate([high, (a - high.astype(F32)).astype(BF16)], axis=1)


def sum_x(where, got, keep, away):
    acc = [got[0, h * WIDTH : (h + 1) * WIDTH, :].astype(F32) for h in range(H)]
    for x in range(1, X):
        acc = [acc[h] + got[x, h * WIDTH : (h + 1) * WIDTH, :].astype(F32) for h in range(H)]
    first = where[10] == 0
    keep[...] = jnp.where(first, acc[0], acc[1])
    away[...] = jnp.where(first, acc[1], acc[0]).astype(BF16)


def sum_h(got, keep, came, send):
    total = (keep[...] + came[...].astype(F32)).astype(BF16)
    lags = []
    for f in range(2):
        acc = jnp.zeros((8, 2 * SUB), F32)
        for r in range(BLOCKS // 2):
            acc += got[f * (BLOCKS // 2) + r, SLICE:ROWS, :].astype(F32)
        lags.append(split(acc[:, 0:SUB] + acc[:, SUB:]).astype(F32))
    rows = lax.broadcasted_iota(jnp.int32, (8, WIDTH), 0)
    for z in range(Z):
        send[z, 0:SLICE, :] = total[z * SLICE : (z + 1) * SLICE, :]
        tile = jnp.where(rows == 0, lags[0][z : z + 1, :], jnp.where(rows == 1, lags[1][z : z + 1, :], 0.0))
        send[z, SLICE:ROWS, :] = tile.astype(BF16)


def scale(got, k, v, gk, gv):
    gp = jnp.concatenate([got[r, 0:SLICE, :] for r in range(BLOCKS)], axis=0).astype(F32).T
    gk[...] = (gp * v[...].astype(F32)).astype(BF16)
    gv[...] = (gp * k[...].astype(F32)).astype(BF16)


def collect(where, got, gw_t, gf):
    acc = jnp.zeros((ROWS, WIDTH), F32)
    for z in range(Z):
        acc += got[z].astype(F32)
    gw_t[...] = acc[0:SLICE, :]
    lags = acc[SLICE : SLICE + 2, 0:SUB] + acc[SLICE : SLICE + 2, SUB:]
    out = jnp.zeros((2, SLICE), F32)
    for n in range(4):
        out += jnp.where(where[11] == n, lags[:, n * SLICE : (n + 1) * SLICE], 0.0)
    gf[...] = out


def shift(block, axis, distance, size):
    return lax.ppermute(block, axis, [(i, i + distance) for i in range(size) if 0 <= i + distance < size])


def per_device(q, k, v, filters, weight, gm):
    y, c, x, h = (lax.axis_index(a) for a in ("y", "c", "x", "h"))
    own_filter = x // 2
    square = (WIDTH, TOK)
    pay, p_t, q_t = call(prepare, [((PAY, TOK), BF16), (square, BF16), (square, BF16)], (q, k, v, gm, filters))
    homes = [((y - n) % Y) * C + c for n in range(Y)] + [((y - n) % Y) * C + 1 - c for n in range(Y)]
    where = jnp.stack(homes + [(y * C + c) * 2 + own_filter, own_filter, h, (x * H + h) % 4]).astype(jnp.int32)
    line = [pay] + [lax.ppermute(pay, "y", [(i, (i + n) % Y) for i in range(Y)]) for n in range(1, Y)]
    p_got = lax.all_to_all(p_t.reshape(BLOCKS, SLICE, TOK), PLANE, 0, 0, tiled=True)
    own = jnp.concatenate(line, axis=0)
    other = lax.ppermute(own, "c", [(0, 1), (1, 0)])
    p_prev = shift(p_got.reshape(square), "z", 1, Z)
    gg_t, send, band = call(
        project,
        [(square, F32), ((BLOCKS, 2 * SLICE, TOK), BF16), (((REACH + 1) * TOK, TOK), BF16)],
        (where, own, other, weight, q_t, p_got, p_prev),
        scalars=1,
        scratch=(pltpu.VMEM((TAPS // TOK, TOK), F32), pltpu.VMEM((2 * WIDTH, TOK), BF16)),
    )
    got = lax.all_to_all(send, PLANE, 0, 0, tiled=True)
    gc_next = shift(got[:, SLICE:, :].reshape(square), "z", -1, Z)
    (send,) = call(
        weigh,
        [((X, H * WIDTH, WIDTH), BF16)],
        (where, own, other, got, q_t),
        scalars=1,
        scratch=(pltpu.VMEM((TOK, WIDTH), BF16),),
    )
    got_x = lax.all_to_all(send, "x", 0, 0, tiled=True)
    send, gq = call(
        backward,
        [((BLOCKS, ROWS, TOK), BF16), (square, BF16)],
        (got, gc_next, band, p_got, p_prev, gg_t),
        scratch=(
            pltpu.VMEM((2 * WIDTH, TOK), BF16),
            pltpu.VMEM((2 * WIDTH, TOK), BF16),
            pltpu.VMEM((2 * WIDTH, TOK), BF16),
            pltpu.VMEM((2 * REACH + 1, SUB, SUB), F32),
        ),
    )
    keep, away = call(sum_x, [(square, F32), (square, BF16)], (where, got_x), scalars=1)
    came = lax.ppermute(away, "h", [(0, 1), (1, 0)])
    got = lax.all_to_all(send, PLANE, 0, 0, tiled=True)
    (send,) = call(sum_h, [((Z, ROWS, WIDTH), BF16)], (got, keep, came))
    got_z = lax.all_to_all(send, "z", 0, 0, tiled=True)
    gk, gv = call(scale, [(square, BF16)] * 2, (got, k, v))
    gw_t, gf = call(collect, [((SLICE, WIDTH), F32), ((2, SLICE), F32)], (where, got_z), scalars=1)
    return gq, gk, gv, gw_t.T, gf


def solution(mesh):
    fine = Mesh(mesh.devices.reshape(Z, X, H, Y, C), ("z", "x", "h", "y", "c"))
    seq, dp = SEQ, ("y", "c")
    in_specs = (P(seq, dp), P(seq, dp), P(seq, dp), P(None, dp), P(dp, None), P(seq, dp))
    out_specs = (P(seq, dp), P(seq, dp), P(seq, dp), P(dp, seq), P(dp, seq))
    return jax.shard_map(per_device, mesh=fine, in_specs=in_specs, out_specs=out_specs, check_vma=False)
```

time: 140 us -> 136 us (0.971)
  the two profiles are of different devices: /device:TPU:8 before, /device:TPU:40 now
where the time goes in v2:
time: 136 us; the launch traced here: 135 us
  starting transfers between devices  43.5 us (32%)
  waiting for transfers between devices  35.3 us (26%)
  blocking collectives  32.3 us (24%)
  Pallas kernels  19 us (14%)
  local copies, waits for them, and re-layouts  4.43 us (3%)
    pallas_call x8, Pallas kernels, call(): pl.pallas_call(body, out_shape=[jax.ShapeDtypeStruct(s, t) for s, t in ou...  19 us
    all_to_all x1, blocking collectives, per_device(): got = lax.all_to_all(send, PLANE, 0, 0, tiled=True)  16.2 us
    all_to_all x1, blocking collectives, per_device(): lax.all_to_all(p_t.reshape(BLOCKS, SLICE, TOK), PLANE, 0, 0, tiled=True)  16.1 us
    all_to_all x1, starting transfers between devices, per_device(): got_z = lax.all_to_all(send, 'z', 0, 0, tiled=True)  11.6 us
    ppermute x3, starting transfers between devices, per_device(): lax.ppermute(pay, 'y', [(i, (i + n) % Y) for i in range(Y)])  9.57 us
    all_to_all x1, starting transfers between devices, per_device(): got = lax.all_to_all(send, PLANE, 0, 0, tiled=True)  9.12 us
    ppermute x2, waiting for transfers between devices, shift(): lax.ppermute(block, axis, [(i, i + distance) for i in range(size) if 0 <=...  7.79 us
    ppermute x3, waiting for transfers between devices, per_device(): lax.ppermute(pay, 'y', [(i, (i + n) % Y) for i in range(Y)])  7.76 us
  transfers between devices with their start and end apart: 10, of which 8 were waited for; matrix products, arithmetic and copies ran while one was open for 1% of the time, Pallas kernels for 5%

profile of v2, /device:TPU:40, one launch (start us, length us, event | category | flops | bytes accessed | tf_op | source)
XLA Modules:
  0.0 135.4 jit_solution(270819759027643195)
XLA Ops:
  0.6 1.9 %prepare.1 = (bf16[272,256]{1,0:T(8,128)(2,1)}, bf16[256,256]{1,0:T(8,128)(2,1)}, bf16[256,256]{1,0:T(8,128)(2,1)}) custom-call(bf16[256,256]{1,0:T(8,128)(2,1)} %q.1, bf16[256,256]{1,0:T(8,128)(2,1)} %k.3, bf16[256,256]{1,0:T(8,128)(2,1)} %v.3, bf16[256,256]{1,0:T(8,128)(2,1)} %gm.1, bf16[16,256]{1,0:T(8,128)(2,1)} %filters.1), custom_call_target="tpu_custom_call" | custom-call | tf_op jit(solution)/shard_map/prepare/pallas_call | solution.py:40
  2.6 2.7 %collective-permute-start = (bf16[272,256]{1,0:T(8,128)(2,1)}, bf16[272,256]{1,0:T(8,128)(2,1)S(1)}, u32[]{:S(2)}, u32[]{:S(2)}) collective-permute-start(bf16[272,256]{1,0:T(8,128)(2,1)} %get-tuple-element.19), channel_id=1, source_target_pairs={{0,2},{2,4},{4,6},{6,0},{1,3},{3,5},{5,7},{7,1},{8,10},{10,12},{12... | collective-permute-start | bytes 417800 | tf_op jit(solution)/shard_map/ppermute | solution.py:217
  5.3 4.9 %collective-permute-start.1 = (bf16[272,256]{1,0:T(8,128)(2,1)}, bf16[272,256]{1,0:T(8,128)(2,1)S(1)}, u32[]{:S(2)}, u32[]{:S(2)}) collective-permute-start(bf16[272,256]{1,0:T(8,128)(2,1)} %get-tuple-element.19), channel_id=1, source_target_pairs={{0,4},{2,6},{4,0},{6,2},{1,5},{3,7},{5,1},{7,3},{8,12},{10,14},{12... | collective-permute-start | bytes 417800 | tf_op jit(solution)/shard_map/ppermute | solution.py:217
  10.2 1.9 %collective-permute-start.2 = (bf16[272,256]{1,0:T(8,128)(2,1)}, bf16[272,256]{1,0:T(8,128)(2,1)S(1)}, u32[]{:S(2)}, u32[]{:S(2)}) collective-permute-start(bf16[272,256]{1,0:T(8,128)(2,1)} %get-tuple-element.19), channel_id=1, source_target_pairs={{0,6},{2,0},{4,2},{6,4},{1,7},{3,1},{5,3},{7,5},{8,14},{10,8},{12,... | collective-permute-start | bytes 417800 | tf_op jit(solution)/shard_map/ppermute | solution.py:217
  12.2 0.9 constant_dynamic-update-slice_fusion.3
  13.1 5.1 %collective-permute-done.1 = bf16[272,256]{1,0:T(8,128)(2,1)S(1)} collective-permute-done((bf16[272,256]{1,0:T(8,128)(2,1)}, bf16[272,256]{1,0:T(8,128)(2,1)S(1)}, u32[]{:S(2)}, u32[]{:S(2)}) %collective-permute-start.1) | collective-permute-done | bytes 139296 | tf_op jit(solution)/shard_map/ppermute | solution.py:217
  18.3 2.6 %collective-permute-done.2 = bf16[272,256]{1,0:T(8,128)(2,1)S(1)} collective-permute-done((bf16[272,256]{1,0:T(8,128)(2,1)}, bf16[272,256]{1,0:T(8,128)(2,1)S(1)}, u32[]{:S(2)}, u32[]{:S(2)}) %collective-permute-start.2) | collective-permute-done | bytes 139296 | tf_op jit(solution)/shard_map/ppermute | solution.py:217
  20.9 1.9 %collective-permute-start.3 = (bf16[1088,256]{1,0:T(8,128)(2,1)S(1)}, bf16[1088,256]{1,0:T(8,128)(2,1)S(1)}, u32[]{:S(2)}, u32[]{:S(2)}) collective-permute-start(bf16[1088,256]{1,0:T(8,128)(2,1)S(1)} %constant_dynamic-update-slice_fusion.own), channel_id=1, source_target_pairs={{0,1},{1,0},{2,3},{3,2},{4,5},{5,4},{6,7},{7,6},{8,9},{9,8},{10,11... | collective-permute-start | bytes 1671176 | tf_op jit(solution)/shard_map/ppermute | solution.py:220
  22.9 16.1 %all_to_all.25.p_got = bf16[8,32,256]{2,1,0:T(8,128)(2,1)S(1)} all-to-all(bf16[8,32,256]{2,1,0:T(8,128)(2,1)S(1)} %bitcast.17), channel_id=1, replica_groups=mesh['z'=8,'x'=4,'h'=2,'y'=4,'c'=2] {'x','h'}, dimensions={0} | all-to-all | bytes 262144 | tf_op jit(solution)/shard_map/all_to_all | solution.py:218
  38.9 4.3 %collective-permute-start.4 = (bf16[256,256]{1,0:T(8,128)(2,1)S(1)}, bf16[256,256]{1,0:T(8,128)(2,1)S(1)}, u32[]{:S(2)}, u32[]{:S(2)}) collective-permute-start(bf16[256,256]{1,0:T(8,128)(2,1)S(1)} %bitcast.16), channel_id=1, source_target_pairs={{0,64},{64,128},{128,192},{192,256},{256,320},{320,384},{384,448},... | collective-permute-start | bytes 393224 | tf_op jit(solution)/shard_map/ppermute | solution.py:207
  43.9 1.8 %collective-permute-done.4.p_prev = bf16[256,256]{1,0:T(8,128)(2,1)S(1)} collective-permute-done((bf16[256,256]{1,0:T(8,128)(2,1)S(1)}, bf16[256,256]{1,0:T(8,128)(2,1)S(1)}, u32[]{:S(2)}, u32[]{:S(2)}) %collective-permute-start.4) | collective-permute-done | bytes 131104 | tf_op jit(solution)/shard_map/ppermute | solution.py:207
  46.5 3.7 %project.1 = (f32[256,256]{1,0:T(8,128)}, bf16[8,64,256]{2,1,0:T(8,128)(2,1)}, bf16[2304,256]{1,0:T(8,128)(2,1)}) custom-call(s32[12]{0:T(128)} %stack.51.where, bf16[1088,256]{1,0:T(8,128)(2,1)} %copy-done.2, bf16[1088,256]{1,0:T(8,128)(2,1)} %copy-done.3, bf16[256,2048]{1,0:T(8,128)(2,1)} %weight.1, bf16[256,256]{1,0:T(8,128)(2,1)} %get-tuple-element.20.q_t, ...), custom_call_target="tpu_custom_call" | custom-call | tf_op jit(solution)/shard_map/project/pallas_call | solution.py:40
  50.2 16.2 %all_to_all.26.got = bf16[8,64,256]{2,1,0:T(8,128)(2,1)} all-to-all(bf16[8,64,256]{2,1,0:T(8,128)(2,1)} %get-tuple-element.22), channel_id=1, replica_groups=mesh['z'=8,'x'=4,'h'=2,'y'=4,'c'=2] {'x','h'}, dimensions={0} | all-to-all | bytes 524288 | tf_op jit(solution)/shard_map/all_to_all | solution.py:229
  66.5 2.8 %weigh.1 = bf16[4,512,256]{2,1,0:T(8,128)(2,1)} custom-call(s32[12]{0:T(128)} %stack.51.where, bf16[1088,256]{1,0:T(8,128)(2,1)} %copy-done.2, bf16[1088,256]{1,0:T(8,128)(2,1)} %copy-done.3, bf16[8,64,256]{2,1,0:T(8,128)(2,1)} %all_to_all.26.got, bf16[256,256]{1,0:T(8,128)(2,1)} %get-tuple-element.20.q_t), custom_call_target="tpu_custom_call" | custom-call | tf_op jit(solution)/shard_map/weigh/pallas_call | solution.py:40
  69.2 3.6 %all-to-all-start.3 = ((bf16[4,512,256]{2,1,0:T(8,128)(2,1)}), bf16[4,512,256]{2,1,0:T(8,128)(2,1)S(1)}, u32[]{:S(2)}, u32[]{:S(2)}) async-start(bf16[4,512,256]{2,1,0:T(8,128)(2,1)} %weigh.1), calls=%async_computation.3 | async-start | bytes 2097152 | tf_op jit(solution)/shard_map/all_to_all | solution.py:238
  72.9 1.3 collective-permute-start.5
  74.2 6.0 %collective-permute-done.5.gc_next = bf16[256,256]{1,0:T(8,128)(2,1)S(1)} collective-permute-done((bf16[256,256]{1,0:T(8,128)(2,1)S(1)}, bf16[256,256]{1,0:T(8,128)(2,1)S(1)}, u32[]{:S(2)}, u32[]{:S(2)}) %collective-permute-start.5) | collective-permute-done | bytes 131104 | tf_op jit(solution)/shard_map/ppermute | solution.py:207
  80.3 0.7 copy-done.8
  80.9 3.3 %backward.1 = (bf16[8,40,256]{2,1,0:T(8,128)(2,1)}, bf16[256,256]{1,0:T(8,128)(2,1)}) custom-call(bf16[8,64,256]{2,1,0:T(8,128)(2,1)} %all_to_all.26.got, bf16[256,256]{1,0:T(8,128)(2,1)} %copy-done.8, bf16[2304,256]{1,0:T(8,128)(2,1)} %get-tuple-element.23.band, bf16[8,32,256]{2,1,0:T(8,128)(2,1)} %copy-done.5, bf16[256,256]{1,0:T(8,128)(2,1)} %copy-done.7, ...), custom_call_target="tpu_custom_call" | custom-call | tf_op jit(solution)/shard_map/backward/pallas_call | solution.py:40
  84.2 3.3 %all-to-all-done.3.got = bf16[4,512,256]{2,1,0:T(8,128)(2,1)S(1)} async-done(((bf16[4,512,256]{2,1,0:T(8,128)(2,1)}), bf16[4,512,256]{2,1,0:T(8,128)(2,1)S(1)}, u32[]{:S(2)}, u32[]{:S(2)}) %all-to-all-start.3) | async-done | bytes 1048608 | tf_op jit(solution)/shard_map/all_to_all | solution.py:238
  87.5 9.1 %all-to-all-start.2 = ((bf16[8,40,256]{2,1,0:T(8,128)(2,1)}), bf16[8,40,256]{2,1,0:T(8,128)(2,1)S(1)}, u32[]{:S(2)}, u32[]{:S(2)}) async-start(bf16[8,40,256]{2,1,0:T(8,128)(2,1)} %get-tuple-element.26), calls=%async_computation.2 | async-start | bytes 327680 | tf_op jit(solution)/shard_map/all_to_all | solution.py:252
  96.6 2.1 %sum_x.1 = (f32[256,256]{1,0:T(8,128)}, bf16[256,256]{1,0:T(8,128)(2,1)}) custom-call(s32[12]{0:T(128)} %stack.51.where, bf16[4,512,256]{2,1,0:T(8,128)(2,1)} %copy-done), custom_call_target="tpu_custom_call" | custom-call | tf_op jit(solution)/shard_map/sum_x/pallas_call | solution.py:40
  98.7 2.0 %collective-permute-start.6 = (bf16[256,256]{1,0:T(8,128)(2,1)}, bf16[256,256]{1,0:T(8,128)(2,1)S(1)}, u32[]{:S(2)}, u32[]{:S(2)}) collective-permute-start(bf16[256,256]{1,0:T(8,128)(2,1)} %get-tuple-element.30), channel_id=1, source_target_pairs={{0,8},{8,0},{1,9},{9,1},{2,10},{10,2},{3,11},{11,3},{4,12},{12,4},... | collective-permute-start | bytes 393224 | tf_op jit(solution)/shard_map/ppermute | solution.py:251
  100.7 2.8 %all-to-all-done.2.got = bf16[8,40,256]{2,1,0:T(8,128)(2,1)S(1)} async-done(((bf16[8,40,256]{2,1,0:T(8,128)(2,1)}), bf16[8,40,256]{2,1,0:T(8,128)(2,1)S(1)}, u32[]{:S(2)}, u32[]{:S(2)}) %all-to-all-start.2) | async-done | bytes 163872 | tf_op jit(solution)/shard_map/all_to_all | solution.py:252
  103.5 6.1 %collective-permute-done.6.came = bf16[256,256]{1,0:T(8,128)(2,1)S(1)} collective-permute-done((bf16[256,256]{1,0:T(8,128)(2,1)}, bf16[256,256]{1,0:T(8,128)(2,1)S(1)}, u32[]{:S(2)}, u32[]{:S(2)}) %collective-permute-start.6) | collective-permute-done | bytes 131104 | tf_op jit(solution)/shard_map/ppermute | solution.py:251
  109.7 0.7 copy-done.10
  110.3 1.8 %sum_h.1 = bf16[8,40,256]{2,1,0:T(8,128)(2,1)} custom-call(bf16[8,40,256]{2,1,0:T(8,128)(2,1)} %copy-done.4, f32[256,256]{1,0:T(8,128)} %get-tuple-element.29.keep, bf16[256,256]{1,0:T(8,128)(2,1)} %copy-done.10), custom_call_target="tpu_custom_call" | custom-call | tf_op jit(solution)/shard_map/sum_h/pallas_call | solution.py:40
  112.1 11.6 %all-to-all-start.4 = ((bf16[8,40,256]{2,1,0:T(8,128)(2,1)}), bf16[8,40,256]{2,1,0:T(8,128)(2,1)S(1)}, u32[]{:S(2)}, u32[]{:S(2)}) async-start(bf16[8,40,256]{2,1,0:T(8,128)(2,1)} %sum_h.1), calls=%async_computation.4 | async-start | bytes 327680 | tf_op jit(solution)/shard_map/all_to_all | solution.py:254
  123.7 1.9 %scale.1 = (bf16[256,256]{1,0:T(8,128)(2,1)}, bf16[256,256]{1,0:T(8,128)(2,1)}) custom-call(bf16[8,40,256]{2,1,0:T(8,128)(2,1)} %copy-done.4, bf16[256,256]{1,0:T(8,128)(2,1)} %k.3, bf16[256,256]{1,0:T(8,128)(2,1)} %v.3), custom_call_target="tpu_custom_call" | custom-call | tf_op jit(solution)/shard_map/scale/pallas_call | solution.py:40
  125.6 7.6 %all-to-all-done.4.got = bf16[8,40,256]{2,1,0:T(8,128)(2,1)S(1)} async-done(((bf16[8,40,256]{2,1,0:T(8,128)(2,1)}), bf16[8,40,256]{2,1,0:T(8,128)(2,1)S(1)}, u32[]{:S(2)}, u32[]{:S(2)}) %all-to-all-start.4) | async-done | bytes 163872 | tf_op jit(solution)/shard_map/all_to_all | solution.py:254
  133.2 0.7 copy-done.6
  133.8 1.6 %collect.1 = (f32[32,256]{1,0:T(8,128)}, f32[2,32]{1,0:T(2,128)}) custom-call(s32[12]{0:T(128)} %stack.51.where, bf16[8,40,256]{2,1,0:T(8,128)(2,1)} %copy-done.6), custom_call_target="tpu_custom_call" | custom-call | tf_op jit(solution)/shard_map/collect/pallas_call | solution.py:40
  (26 shorter events, 1.5 us)
Async XLA Ops:
  2.6 20.3 %copy-start.9 = (bf16[256,256]{1,0:T(8,128)(2,1)S(1)}, bf16[256,256]{1,0:T(8,128)(2,1)}, u32[]{:S(2)}) copy-start(bf16[256,256]{1,0:T(8,128)(2,1)} %get-tuple-element.21) | copy-start | bytes 393220
  2.6 10.5 %collective-permute-start = (bf16[272,256]{1,0:T(8,128)(2,1)}, bf16[272,256]{1,0:T(8,128)(2,1)S(1)}, u32[]{:S(2)}, u32[]{:S(2)}) collective-permute-start(bf16[272,256]{1,0:T(8,128)(2,1)} %get-tuple-element.19), channel_id=1, source_target_pairs={{0,2},{2,4},{4,6},{6,0},{1,3},{3,5},{5,7},{7,1},{8,10},{10,12},{12... | collective-permute-start | bytes 417800 | tf_op jit(solution)/shard_map/ppermute | solution.py:217
  5.3 13.0 %collective-permute-start.1 = (bf16[272,256]{1,0:T(8,128)(2,1)}, bf16[272,256]{1,0:T(8,128)(2,1)S(1)}, u32[]{:S(2)}, u32[]{:S(2)}) collective-permute-start(bf16[272,256]{1,0:T(8,128)(2,1)} %get-tuple-element.19), channel_id=1, source_target_pairs={{0,4},{2,6},{4,0},{6,2},{1,5},{3,7},{5,1},{7,3},{8,12},{10,14},{12... | collective-permute-start | bytes 417800 | tf_op jit(solution)/shard_map/ppermute | solution.py:217
  10.2 10.7 %collective-permute-start.2 = (bf16[272,256]{1,0:T(8,128)(2,1)}, bf16[272,256]{1,0:T(8,128)(2,1)S(1)}, u32[]{:S(2)}, u32[]{:S(2)}) collective-permute-start(bf16[272,256]{1,0:T(8,128)(2,1)} %get-tuple-element.19), channel_id=1, source_target_pairs={{0,6},{2,0},{4,2},{6,4},{1,7},{3,1},{5,3},{7,5},{8,14},{10,8},{12,... | collective-permute-start | bytes 417800 | tf_op jit(solution)/shard_map/ppermute | solution.py:217
  20.9 24.8 %copy-start.2 = (bf16[1088,256]{1,0:T(8,128)(2,1)}, bf16[1088,256]{1,0:T(8,128)(2,1)S(1)}, u32[]{:S(2)}) copy-start(bf16[1088,256]{1,0:T(8,128)(2,1)S(1)} %constant_dynamic-update-slice_fusion.own) | copy-start | bytes 1671172
  20.9 24.8 %collective-permute-start.3 = (bf16[1088,256]{1,0:T(8,128)(2,1)S(1)}, bf16[1088,256]{1,0:T(8,128)(2,1)S(1)}, u32[]{:S(2)}, u32[]{:S(2)}) collective-permute-start(bf16[1088,256]{1,0:T(8,128)(2,1)S(1)} %constant_dynamic-update-slice_fusion.own), channel_id=1, source_target_pairs={{0,1},{1,0},{2,3},{3,2},{4,5},{5,4},{6,7},{7,6},{8,9},{9,8},{10,11... | collective-permute-start | bytes 1671176 | tf_op jit(solution)/shard_map/ppermute | solution.py:220
  38.9 6.8 %copy-start.5 = (bf16[8,32,256]{2,1,0:T(8,128)(2,1)}, bf16[8,32,256]{2,1,0:T(8,128)(2,1)S(1)}, u32[]{:S(2)}) copy-start(bf16[8,32,256]{2,1,0:T(8,128)(2,1)S(1)} %all_to_all.25.p_got) | copy-start | bytes 393220
  38.9 6.8 %collective-permute-start.4 = (bf16[256,256]{1,0:T(8,128)(2,1)S(1)}, bf16[256,256]{1,0:T(8,128)(2,1)S(1)}, u32[]{:S(2)}, u32[]{:S(2)}) collective-permute-start(bf16[256,256]{1,0:T(8,128)(2,1)S(1)} %bitcast.16), channel_id=1, source_target_pairs={{0,64},{64,128},{128,192},{192,256},{256,320},{320,384},{384,448},... | collective-permute-start | bytes 393224 | tf_op jit(solution)/shard_map/ppermute | solution.py:207
  45.7 0.6 copy-start.7
  45.7 0.8 copy-start.3
  69.2 3.7 %copy-start.1 = (bf16[8,64,256]{2,1,0:T(8,128)(2,1)S(1)}, bf16[8,64,256]{2,1,0:T(8,128)(2,1)}, u32[]{:S(2)}) copy-start(bf16[8,64,256]{2,1,0:T(8,128)(2,1)} %all_to_all.26.got) | copy-start | bytes 786436
  69.2 18.2 %all-to-all-start.3 = ((bf16[4,512,256]{2,1,0:T(8,128)(2,1)}), bf16[4,512,256]{2,1,0:T(8,128)(2,1)S(1)}, u32[]{:S(2)}, u32[]{:S(2)}) async-start(bf16[4,512,256]{2,1,0:T(8,128)(2,1)} %weigh.1), calls=%async_computation.3 | async-start | bytes 2097152 | tf_op jit(solution)/shard_map/all_to_all | solution.py:238
  72.9 7.3 %collective-permute-start.5 = (bf16[256,256]{1,0:T(8,128)(2,1)S(1)}, bf16[256,256]{1,0:T(8,128)(2,1)S(1)}, u32[]{:S(2)}, u32[]{:S(2)}) collective-permute-start(bf16[256,256]{1,0:T(8,128)(2,1)S(1)} %bitcast.18), channel_id=1, source_target_pairs={{64,0},{128,64},{192,128},{256,192},{320,256},{384,320},{448,384},... | collective-permute-start | bytes 393224 | tf_op jit(solution)/shard_map/ppermute | solution.py:207
  80.3 0.7 copy-start.8
  87.5 9.1 %copy-start = (bf16[4,512,256]{2,1,0:T(8,128)(2,1)}, bf16[4,512,256]{2,1,0:T(8,128)(2,1)S(1)}, u32[]{:S(2)}) copy-start(bf16[4,512,256]{2,1,0:T(8,128)(2,1)S(1)} %all-to-all-done.3.got) | copy-start | bytes 3145732
  87.5 16.1 %all-to-all-start.2 = ((bf16[8,40,256]{2,1,0:T(8,128)(2,1)}), bf16[8,40,256]{2,1,0:T(8,128)(2,1)S(1)}, u32[]{:S(2)}, u32[]{:S(2)}) async-start(bf16[8,40,256]{2,1,0:T(8,128)(2,1)} %get-tuple-element.26), calls=%async_computation.2 | async-start | bytes 327680 | tf_op jit(solution)/shard_map/all_to_all | solution.py:252
  98.7 11.0 %collective-permute-start.6 = (bf16[256,256]{1,0:T(8,128)(2,1)}, bf16[256,256]{1,0:T(8,128)(2,1)S(1)}, u32[]{:S(2)}, u32[]{:S(2)}) collective-permute-start(bf16[256,256]{1,0:T(8,128)(2,1)} %get-tuple-element.30), channel_id=1, source_target_pairs={{0,8},{8,0},{1,9},{9,1},{2,10},{10,2},{3,11},{11,3},{4,12},{12,4},... | collective-permute-start | bytes 393224 | tf_op jit(solution)/shard_map/ppermute | solution.py:251
  103.5 6.1 %copy-start.4 = (bf16[8,40,256]{2,1,0:T(8,128)(2,1)}, bf16[8,40,256]{2,1,0:T(8,128)(2,1)S(1)}, u32[]{:S(2)}) copy-start(bf16[8,40,256]{2,1,0:T(8,128)(2,1)S(1)} %all-to-all-done.2.got) | copy-start | bytes 491524
  109.7 0.7 copy-start.10
  112.1 21.1 %all-to-all-start.4 = ((bf16[8,40,256]{2,1,0:T(8,128)(2,1)}), bf16[8,40,256]{2,1,0:T(8,128)(2,1)S(1)}, u32[]{:S(2)}, u32[]{:S(2)}) async-start(bf16[8,40,256]{2,1,0:T(8,128)(2,1)} %sum_h.1), calls=%async_computation.4 | async-start | bytes 327680 | tf_op jit(solution)/shard_map/all_to_all | solution.py:254
  133.1 0.7 copy-start.6
